TPU v7x, 128 devices: a whole 4x4x4 slice. The times are simulated.
128 devices in a mesh: segment: 4 (over y), lane: 32 (over x, z, core).
Axes of the slice: x: 4, y: 4, z: 4, core: 2. Of those that a mesh axis runs over, the one named last changes fastest.
Arguments:
- frames: bfloat16 [96, 197, 1024], P('lane'), may hold values from -6 to 6
- triple_weight: bfloat16 [4, 1024, 3072], P('segment'), as said below
- output_weight: bfloat16 [4, 1024, 1024], P('segment'), may hold values from -0.1875 to 0.1875
- expand_weight: bfloat16 [4, 1024, 4096], P('segment', None, 'lane'), may hold values from -0.1875 to 0.1875
- reduce_weight: bfloat16 [4, 4096, 1024], P('segment', 'lane'), may hold values from -0.09375 to 0.09375
- attend_gain: float32 [4, 1024], P('segment'), may hold values from 0.1 to 1.9
- dense_gain: float32 [4, 1024], P('segment'), may hold values from 0.1 to 1.9
- final_gain: float32 [1024], replicated, may hold values from 0.1 to 1.9
- shot_lengths: int32 [24], replicated, may hold values from 1 to 12, as said below
Outputs:
- shot_frames: float32 [96, 1024], P('lane', 'segment')
Inputs may be any that keep to these rules, and one draw needn't show every extreme that they name: `shot_lengths`: each shot is a run of consecutive frames; the lengths sum to 96; the first shot has 2 frames and the second exactly 12. `triple_weight`: query and value columns are drawn like a weight with fan-in 1024; key columns may be up to 60 times that scale and correlated with the query columns.
All inputs are finite; a program needn't handle non-finite values.
Results may differ from a plain program's by a relative error of at most 0.023.
Values may be sent and summed in bfloat16 or wider, within the bound.
A program may use at most 128 MiB of HBM per device.

v0:
```python
import math
import jax
import jax.numpy as jnp
from jax import lax
from jax.sharding import PartitionSpec as P

HEADS = 16
MOST = 12


def from_behind(value, axis, steps):
    count = lax.axis_size(axis)
    leading, last = (max(0, -steps), min(count, count - steps))
    return lax.ppermute(value, axis, [(source, source + steps) for source in range(leading, last)])


def normalize(states, gain_row):
    average = jnp.mean(states, axis=-1, keepdims=True)
    centred = states - average
    spread = jnp.mean(centred * centred, axis=-1, keepdims=True)
    return centred * lax.rsqrt(spread + 1e-06) * gain_row


def spatial_layer(
    states, triple_weight, output_weight, expand_weight, reduce_weight, attend_gain, dense_gain
):
    group_size, row_count, model_width = states.shape
    head_size = model_width // HEADS
    normed = normalize(states, attend_gain).astype(jnp.bfloat16)
    packed = jnp.einsum(
        "gpd,de->gpe", normed, triple_weight, preferred_element_type=jnp.float32
    ).astype(jnp.bfloat16)
    packed = packed.reshape(group_size, row_count, 3, HEADS, head_size)
    scores = jnp.einsum(
        "gqhe,gkhe->ghqk", packed[:, :, 0], packed[:, :, 1], preferred_element_type=jnp.float32
    ) / math.sqrt(head_size)
    weights = jax.nn.softmax(scores, axis=-1).astype(jnp.bfloat16)
    context = jnp.einsum(
        "ghqk,gkhe->gqhe", weights, packed[:, :, 2], preferred_element_type=jnp.float32
    )
    context = context.astype(jnp.bfloat16).reshape(group_size, row_count, model_width)
    states = states + jnp.einsum(
        "gpd,de->gpe", context, output_weight, preferred_element_type=jnp.float32
    )
    normed = normalize(states, dense_gain).astype(jnp.bfloat16)
    hidden = jax.nn.gelu(
        jnp.einsum("gpd,df->gpf", normed, expand_weight, preferred_element_type=jnp.float32),
        approximate=False,
    ).astype(jnp.bfloat16)
    return states + jnp.einsum(
        "gpf,fd->gpd", hidden, reduce_weight, preferred_element_type=jnp.float32
    )


def shot_number(positions, shot_ends):
    return jnp.sum((shot_ends[None, :] <= positions[:, None]).astype(jnp.int32), axis=1)


def fold_keys(running, portion, first_row, queries, query_shot, shot_ends, frame_total):
    highest, totals, weighted = running
    row_count = portion.shape[0]
    model_width = portion.shape[1] // 2
    head_size = model_width // HEADS
    key_rows = portion[:, :model_width].reshape(row_count, HEADS, head_size)
    value_rows = portion[:, model_width:].astype(jnp.float32).reshape(row_count, HEADS, head_size)
    positions = first_row + jnp.arange(row_count, dtype=jnp.int32)
    inside = (positions >= 0) & (positions < frame_total)
    allowed = (query_shot[:, None] == shot_number(positions, shot_ends)[None, :]) & inside[None, :]
    scores = jnp.einsum(
        "qhe,khe->hqk", queries, key_rows, preferred_element_type=jnp.float32
    ) / math.sqrt(head_size)
    masked = jnp.where(allowed[None], scores, -1e30)
    raised = jnp.maximum(highest, jnp.max(masked, axis=-1))
    factor = jnp.exp(highest - raised)
    shares = jnp.where(allowed[None], jnp.exp(scores - raised[:, :, None]), 0.0)
    totals = totals * factor + jnp.sum(shares, axis=-1)
    weighted = weighted * jnp.transpose(factor)[:, :, None] + jnp.einsum(
        "hqk,khe->qhe", shares, value_rows, precision=lax.Precision.HIGHEST
    )
    return (raised, totals, weighted)


def body(
    frames,
    triple_weight,
    output_weight,
    expand_weight,
    reduce_weight,
    attend_gain,
    dense_gain,
    final_gain,
    shot_lengths,
):
    segment_index = lax.axis_index("segment")
    segment_count = lax.axis_size("segment")
    lane_index = lax.axis_index("lane")
    lane_count = lax.axis_size("lane")
    frame_count, row_count, model_width = frames.shape
    expand_full, reduce_full = (
        lax.all_gather(expand_weight[0], "lane", axis=1, tiled=True),
        lax.all_gather(reduce_weight[0], "lane", axis=0, tiled=True),
    )
    triple_local = triple_weight[0]
    output_local = output_weight[0]
    attend_local = attend_gain[0]
    dense_local = dense_gain[0]
    group_size = 1
    micro_count = frame_count // group_size

    def advance(moment, running):
        current, pooled = running
        first_frame = jnp.minimum(moment, micro_count - 1) * group_size
        loaded = lax.dynamic_slice_in_dim(frames, first_frame, group_size, 0).astype(jnp.float32)
        current = jnp.where(segment_index == 0, loaded, current)
        result = spatial_layer(
            current, triple_local, output_local, expand_full, reduce_full, attend_local, dense_local
        )
        arrived = from_behind(result, "segment", 1)
        finished = moment - (segment_count - 2)
        summary = jnp.mean(normalize(arrived, final_gain), axis=1)
        slot_row = jnp.clip(finished, 0, micro_count - 1) * group_size
        previous = lax.dynamic_slice_in_dim(pooled, slot_row, group_size, 0)
        updated = jnp.where(finished >= 0, summary, previous)
        return (arrived, lax.dynamic_update_slice_in_dim(pooled, updated, slot_row, 0))

    start_state = (
        jnp.zeros((group_size, row_count, model_width), jnp.float32),
        jnp.zeros((frame_count, model_width), jnp.float32),
    )
    settled, pooled = lax.fori_loop(0, micro_count + segment_count - 2, advance, start_state)
    head_size = model_width // HEADS
    normed = normalize(pooled, attend_local).astype(jnp.bfloat16)
    packed = jnp.dot(normed, triple_local, preferred_element_type=jnp.float32).astype(jnp.bfloat16)
    queries = packed[:, :model_width].reshape(frame_count, HEADS, head_size)
    key_value = packed[:, model_width:]
    shot_ends = jnp.cumsum(shot_lengths)
    frame_total = frame_count * lane_count
    own_rows = lane_index * frame_count + jnp.arange(frame_count, dtype=jnp.int32)
    query_shot = shot_number(own_rows, shot_ends)

    def absorb(running, portion, first_row):
        return fold_keys(running, portion, first_row, queries, query_shot, shot_ends, frame_total)

    empty = (
        jnp.full((HEADS, frame_count), -1e30, jnp.float32),
        jnp.zeros((HEADS, frame_count), jnp.float32),
        jnp.zeros((frame_count, HEADS, head_size), jnp.float32),
    )
    running = absorb(empty, key_value, lane_index * frame_count)
    reach = (MOST + frame_count - 2) // frame_count
    offsets = [direction * distance for distance in range(1, reach + 1) for direction in (1, -1)]
    for offset in offsets:
        portion = from_behind(key_value, "lane", offset)
        running = absorb(running, portion, (lane_index - offset) * frame_count)
    highest, totals, weighted = running
    context = (
        (weighted / jnp.transpose(totals)[:, :, None])
        .reshape(frame_count, model_width)
        .astype(jnp.bfloat16)
    )
    temporal = pooled + jnp.dot(context, output_local, preferred_element_type=jnp.float32)
    normed = normalize(temporal, dense_local).astype(jnp.bfloat16)
    hidden = jax.nn.gelu(
        jnp.dot(normed, expand_full, preferred_element_type=jnp.float32), approximate=False
    ).astype(jnp.bfloat16)
    temporal = temporal + jnp.dot(hidden, reduce_full, preferred_element_type=jnp.float32)
    columns = temporal.reshape(frame_count, segment_count, model_width // segment_count)
    shared = lax.all_to_all(columns, "segment", split_axis=1, concat_axis=1, tiled=True)
    return shared[:, segment_count - 1]


def solution(mesh):
    return jax.shard_map(
        body,
        mesh=mesh,
        in_specs=(
            P("lane", None, None),
            P("segment", None, None),
            P("segment", None, None),
            P("segment", None, "lane"),
            P("segment", "lane", None),
            P("segment", None),
            P("segment", None),
            P(),
            P(),
        ),
        out_specs=P("lane", "segment"),
        check_vma=False,
    )
```

profile of v0, /device:TPU:2, one launch (start us, length us, event | category | flops | bytes accessed | tf_op | source)
XLA Modules:
  0.0 478.3 jit_solution(12670992070367799868)
XLA Ops:
  10.1 61.2 %all-gather.5.cloned.1.call-done = bf16[1,1024,4096]{2,1,0:T(8,128)(2,1)} async-done(((bf16[1,1024,128]{2,1,0:T(8,128)(2,1)}), bf16[1,1024,4096]{2,1,0:T(8,128)(2,1)}) %all-gather.5.cloned.1.call-update) | async-done | bytes 8388624 | tf_op jit(solution)/shard_map/all_gather | solution.py:100
  71.3 55.2 %all-gather.7.cloned.1.call-done = bf16[1,4096,1024]{2,1,0:T(8,128)(2,1)} async-done(((bf16[1,128,1024]{2,1,0:T(8,128)(2,1)}), bf16[1,4096,1024]{2,1,0:T(8,128)(2,1)}) %all-gather.7.cloned.1.call-update) | async-done | bytes 8388624 | tf_op jit(solution)/shard_map/all_gather | solution.py:101
  127.0 283.0 %while.17 = (s32[]{:T(128)}, f32[1,197,1024]{2,0,1:T(1,128)S(1)}, f32[3,1024]{1,0:T(4,128)S(1)}, pred[]{:T(512)}, bf16[3,197,1024]{2,1,0:T(8,128)(2,1)}, /*index...) while((s32[]{:T(128)}, f32[1,197,1024]{2,0,1:T(1,128)S(1)}, ...), condition=%wide.region_10.11_spmd, body=%wide.region_0.10_spmd.sunk | while | flops 5180471808 | bytes 65759924 | solution.py:130
  128.2 1.3 multiply_reduce_fusion.11
  129.5 5.6 %convolution_convert_fusion.3 = bf16[197,3072]{1,0:T(8,128)(2,1)} fusion(bf16[1024,3072]{1,0:T(8,128)(2,1)} %get-tuple-element.539, f32[1024]{0:T(1024)} %bitcast.303, f32[197]{0:T(256)S(1)} %add_rsqrt_fusion.8, f32[197]{0:T(256)S(1)} %broadcast_multiply_fusion.10, f32[1,197,1024]{2,0,1:T(1,128)S(1)} %get-tuple-element.516, ...), kind=kOutput, calls=%fused_computation.2.clone.1 | convolution fusion | flops 1241232384 | bytes 8724524 | tf_op jit(solution)/shard_map/while/body/eval_jaxpr/gpd,de->gpe/dot_general | solution.py:30
  135.1 1.6 copy.297
  137.4 2.7 fusion.341
  141.7 1.7 fusion.343
  143.7 14.2 %fusion.344 = f32[1,197,1024]{2,1,0:T(8,128)S(1)} fusion(f32[1,197,1024]{2,1,0:T(8,128)S(1)} %get-tuple-element.495, bf16[4096,1024]{1,0:T(8,128)(2,1)} %get-tuple-element.543, bf16[1024,4096]{1,0:T(8,128)(2,1)} %get-tuple-element.542, f32[1024]{0:T(1024)S(1)} %bitcast.305, f32[197]{0:T(256)S(1)} %add_rsqrt_fusion.9, ...), kind=kOutput, calls=%fused_computation.61.clone.1 | convolution fusion | flops 3358569472 | bytes 18396712 | tf_op jit(solution)/shard_map/while/body/eval_jaxpr/gpf,fd->gpd/dot_general | solution.py:50
  158.8 3.4 collective-permute-start
  162.2 17.6 %collective-permute-done = f32[1,197,1024]{2,0,1:T(1,128)S(1)} collective-permute-done((f32[1,197,1024]{2,0,1:T(1,128)S(1)}, f32[1,197,1024]{2,0,1:T(1,128)S(1)}, u32[]{:S(2)}, u32[]{:S(2)}) %collective-permute-start) | collective-permute-done | bytes 806944 | tf_op jit(solution)/shard_map/while/body/eval_jaxpr/ppermute | solution.py:14
  180.9 2.1 multiply_reduce_fusion.13
  183.0 1.3 multiply_reduce_fusion.14
  185.7 1.3 multiply_reduce_fusion.11
  187.0 5.6 %convolution_convert_fusion.3 = bf16[197,3072]{1,0:T(8,128)(2,1)} fusion(bf16[1024,3072]{1,0:T(8,128)(2,1)} %get-tuple-element.539, f32[1024]{0:T(1024)} %bitcast.303, f32[197]{0:T(256)S(1)} %add_rsqrt_fusion.8, f32[197]{0:T(256)S(1)} %broadcast_multiply_fusion.10, f32[1,197,1024]{2,0,1:T(1,128)S(1)} %get-tuple-element.516, ...), kind=kOutput, calls=%fused_computation.2.clone.1 | convolution fusion | flops 1241232384 | bytes 8724524 | tf_op jit(solution)/shard_map/while/body/eval_jaxpr/gpd,de->gpe/dot_general | solution.py:30
  192.6 1.6 copy.297
  194.9 2.7 fusion.341
  199.2 1.7 fusion.343
  201.2 14.2 %fusion.344 = f32[1,197,1024]{2,1,0:T(8,128)S(1)} fusion(f32[1,197,1024]{2,1,0:T(8,128)S(1)} %get-tuple-element.495, bf16[4096,1024]{1,0:T(8,128)(2,1)} %get-tuple-element.543, bf16[1024,4096]{1,0:T(8,128)(2,1)} %get-tuple-element.542, f32[1024]{0:T(1024)S(1)} %bitcast.305, f32[197]{0:T(256)S(1)} %add_rsqrt_fusion.9, ...), kind=kOutput, calls=%fused_computation.61.clone.1 | convolution fusion | flops 3358569472 | bytes 18396712 | tf_op jit(solution)/shard_map/while/body/eval_jaxpr/gpf,fd->gpd/dot_general | solution.py:50
  216.3 4.4 collective-permute-start
  220.7 16.8 %collective-permute-done = f32[1,197,1024]{2,0,1:T(1,128)S(1)} collective-permute-done((f32[1,197,1024]{2,0,1:T(1,128)S(1)}, f32[1,197,1024]{2,0,1:T(1,128)S(1)}, u32[]{:S(2)}, u32[]{:S(2)}) %collective-permute-start) | collective-permute-done | bytes 806944 | tf_op jit(solution)/shard_map/while/body/eval_jaxpr/ppermute | solution.py:14
  238.6 2.1 multiply_reduce_fusion.13
  240.8 1.3 multiply_reduce_fusion.14
  243.4 1.3 multiply_reduce_fusion.11
  244.7 5.6 %convolution_convert_fusion.3 = bf16[197,3072]{1,0:T(8,128)(2,1)} fusion(bf16[1024,3072]{1,0:T(8,128)(2,1)} %get-tuple-element.539, f32[1024]{0:T(1024)} %bitcast.303, f32[197]{0:T(256)S(1)} %add_rsqrt_fusion.8, f32[197]{0:T(256)S(1)} %broadcast_multiply_fusion.10, f32[1,197,1024]{2,0,1:T(1,128)S(1)} %get-tuple-element.516, ...), kind=kOutput, calls=%fused_computation.2.clone.1 | convolution fusion | flops 1241232384 | bytes 8724524 | tf_op jit(solution)/shard_map/while/body/eval_jaxpr/gpd,de->gpe/dot_general | solution.py:30
  250.3 1.6 copy.297
  252.6 2.7 fusion.341
  256.9 1.7 fusion.343
  258.9 14.2 %fusion.344 = f32[1,197,1024]{2,1,0:T(8,128)S(1)} fusion(f32[1,197,1024]{2,1,0:T(8,128)S(1)} %get-tuple-element.495, bf16[4096,1024]{1,0:T(8,128)(2,1)} %get-tuple-element.543, bf16[1024,4096]{1,0:T(8,128)(2,1)} %get-tuple-element.542, f32[1024]{0:T(1024)S(1)} %bitcast.305, f32[197]{0:T(256)S(1)} %add_rsqrt_fusion.9, ...), kind=kOutput, calls=%fused_computation.61.clone.1 | convolution fusion | flops 3358569472 | bytes 18396712 | tf_op jit(solution)/shard_map/while/body/eval_jaxpr/gpf,fd->gpd/dot_general | solution.py:50
  274.0 4.4 collective-permute-start
  278.4 15.9 %collective-permute-done = f32[1,197,1024]{2,0,1:T(1,128)S(1)} collective-permute-done((f32[1,197,1024]{2,0,1:T(1,128)S(1)}, f32[1,197,1024]{2,0,1:T(1,128)S(1)}, u32[]{:S(2)}, u32[]{:S(2)}) %collective-permute-start) | collective-permute-done | bytes 806944 | tf_op jit(solution)/shard_map/while/body/eval_jaxpr/ppermute | solution.py:14
  295.4 2.1 multiply_reduce_fusion.13
  297.5 1.3 multiply_reduce_fusion.14
  301.5 5.6 %convolution_convert_fusion.3 = bf16[197,3072]{1,0:T(8,128)(2,1)} fusion(bf16[1024,3072]{1,0:T(8,128)(2,1)} %get-tuple-element.539, f32[1024]{0:T(1024)} %bitcast.303, f32[197]{0:T(256)S(1)} %add_rsqrt_fusion.8, f32[197]{0:T(256)S(1)} %broadcast_multiply_fusion.10, f32[1,197,1024]{2,0,1:T(1,128)S(1)} %get-tuple-element.516, ...), kind=kOutput, calls=%fused_computation.2.clone.1 | convolution fusion | flops 1241232384 | bytes 8724524 | tf_op jit(solution)/shard_map/while/body/eval_jaxpr/gpd,de->gpe/dot_general | solution.py:30
  307.1 1.6 copy.297
  309.4 2.7 fusion.341
  313.7 1.7 fusion.343
  315.7 14.2 %fusion.344 = f32[1,197,1024]{2,1,0:T(8,128)S(1)} fusion(f32[1,197,1024]{2,1,0:T(8,128)S(1)} %get-tuple-element.495, bf16[4096,1024]{1,0:T(8,128)(2,1)} %get-tuple-element.543, bf16[1024,4096]{1,0:T(8,128)(2,1)} %get-tuple-element.542, f32[1024]{0:T(1024)S(1)} %bitcast.305, f32[197]{0:T(256)S(1)} %add_rsqrt_fusion.9, ...), kind=kOutput, calls=%fused_computation.61.clone.1 | convolution fusion | flops 3358569472 | bytes 18396712 | tf_op jit(solution)/shard_map/while/body/eval_jaxpr/gpf,fd->gpd/dot_general | solution.py:50
  330.8 4.4 collective-permute-start
  335.2 14.9 %collective-permute-done = f32[1,197,1024]{2,0,1:T(1,128)S(1)} collective-permute-done((f32[1,197,1024]{2,0,1:T(1,128)S(1)}, f32[1,197,1024]{2,0,1:T(1,128)S(1)}, u32[]{:S(2)}, u32[]{:S(2)}) %collective-permute-start) | collective-permute-done | bytes 806944 | tf_op jit(solution)/shard_map/while/body/eval_jaxpr/ppermute | solution.py:14
  351.3 2.1 multiply_reduce_fusion.13
  353.4 1.3 multiply_reduce_fusion.14
  357.4 5.6 %convolution_convert_fusion.3 = bf16[197,3072]{1,0:T(8,128)(2,1)} fusion(bf16[1024,3072]{1,0:T(8,128)(2,1)} %get-tuple-element.539, f32[1024]{0:T(1024)} %bitcast.303, f32[197]{0:T(256)S(1)} %add_rsqrt_fusion.8, f32[197]{0:T(256)S(1)} %broadcast_multiply_fusion.10, f32[1,197,1024]{2,0,1:T(1,128)S(1)} %get-tuple-element.516, ...), kind=kOutput, calls=%fused_computation.2.clone.1 | convolution fusion | flops 1241232384 | bytes 8724524 | tf_op jit(solution)/shard_map/while/body/eval_jaxpr/gpd,de->gpe/dot_general | solution.py:30
  363.0 1.6 copy.297
  365.2 2.7 fusion.341
  369.5 1.7 fusion.343
  371.6 14.2 %fusion.344 = f32[1,197,1024]{2,1,0:T(8,128)S(1)} fusion(f32[1,197,1024]{2,1,0:T(8,128)S(1)} %get-tuple-element.495, bf16[4096,1024]{1,0:T(8,128)(2,1)} %get-tuple-element.543, bf16[1024,4096]{1,0:T(8,128)(2,1)} %get-tuple-element.542, f32[1024]{0:T(1024)S(1)} %bitcast.305, f32[197]{0:T(256)S(1)} %add_rsqrt_fusion.9, ...), kind=kOutput, calls=%fused_computation.61.clone.1 | convolution fusion | flops 3358569472 | bytes 18396712 | tf_op jit(solution)/shard_map/while/body/eval_jaxpr/gpf,fd->gpd/dot_general | solution.py:50
  386.6 4.4 collective-permute-start
  391.1 14.0 %collective-permute-done = f32[1,197,1024]{2,0,1:T(1,128)S(1)} collective-permute-done((f32[1,197,1024]{2,0,1:T(1,128)S(1)}, f32[1,197,1024]{2,0,1:T(1,128)S(1)}, u32[]{:S(2)}, u32[]{:S(2)}) %collective-permute-start) | collective-permute-done | bytes 806944 | tf_op jit(solution)/shard_map/while/body/eval_jaxpr/ppermute | solution.py:14
  406.2 2.1 multiply_reduce_fusion.13
  408.3 1.3 multiply_reduce_fusion.14
  410.4 3.8 convolution_convert_fusion.1
  414.2 4.6 collective-permute-start.8
  418.8 2.9 collective-permute-start.7
  421.7 1.9 collective-permute-start.6
  423.6 3.6 collective-permute-start.5
  427.2 7.2 %collective-permute-start.4 = (bf16[3,2048]{1,0:T(4,128)(2,1)S(1)}, bf16[3,2048]{1,0:T(4,128)(2,1)S(1)}, u32[]{:S(2)}, u32[]{:S(2)}) collective-permute-start(bf16[3,2048]{1,0:T(4,128)(2,1)S(1)} %slice.122), channel_id=1, source_target_pairs={{2,0},{3,1},{4,2},{5,3},{6,4},{7,5},{8,6},{9,7},{10,8},{11,9},{12,... | collective-permute-start | bytes 36872 | tf_op jit(solution)/shard_map/ppermute | solution.py:14
  434.9 1.9 collective-permute-start.3
  436.9 2.2 collective-permute-start.2
  439.1 2.2 collective-permute-start.1
  441.3 1.3 collective-permute-done.3
  443.3 3.1 collective-permute-done.1
  452.4 8.1 %convolution_add_fusion = f32[3,1024]{1,0:T(4,128)S(1)} fusion(f32[3,1024]{1,0:T(4,128)S(1)} %get-tuple-element.399, f32[1024]{0:T(1024)S(1)} %bitcast.306, f32[3]{0:T(128)S(1)} %add_rsqrt_fusion.3, f32[3]{0:T(128)S(1)} %broadcast_multiply_fusion.4, bf16[1,4096,1024]{2,1,0:T(8,128)(2,1)} %bitcast.298, bf16[1,1024,4096]{2,1,0:T(8,128)(2,1)} %bitcast.296), kind=kOutput, calls=%fused_computation.161 | convolution fusion | flops 51145728 | bytes 16805912 | tf_op jit(solution)/shard_map/dot_general | solution.py:166
  460.5 10.4 %all_to_all.5 = f32[3,4,256]{2,0,1:T(4,128)S(1)} all-to-all(f32[3,4,256]{2,0,1:T(4,128)S(1)} %bitcast.302), channel_id=1, replica_groups=mesh['segment'=4,'lane'=32] {'segment'}, dimensions={1} | all-to-all | bytes 24576 | tf_op jit(solution)/shard_map/all_to_all | solution.py:168
  (226 shorter events, 42.8 us)
Async XLA Ops:
  6.5 64.8 %all-gather.5.cloned.1.call-start = ((), (), s32[]{:S(2)}) async-start(), calls=%async_computation.1 | async-start | bytes 8650752 | tf_op jit(solution)/shard_map/all_gather | solution.py:100
  7.3 119.3 %all-gather.7.cloned.1.call-start = ((), (), s32[]{:S(2)}) async-start(), calls=%async_computation.2 | async-start | bytes 8650752 | tf_op jit(solution)/shard_map/all_gather | solution.py:101
  140.1 1.6 copy-start
  140.6 3.1 copy-start.3
  143.7 39.3 %copy-start.2 = (f32[1024]{0:T(1024)S(1)}, f32[1024]{0:T(1024)}, u32[]{:S(2)}) copy-start(f32[1024]{0:T(1024)} %get-tuple-element.544) | copy-start | bytes 12292 | tf_op jit(solution)/shard_map/while
  158.8 21.1 %collective-permute-start = (f32[1,197,1024]{2,0,1:T(1,128)S(1)}, f32[1,197,1024]{2,0,1:T(1,128)S(1)}, u32[]{:S(2)}, u32[]{:S(2)}) collective-permute-start(f32[1,197,1024]{2,0,1:T(1,128)S(1)} %copy.298), channel_id=1, source_target_pairs={{0,32},{32,64},{64,96},{1,33},{33,65},{65,97},{2,34},{34,66},{66,9... | collective-permute-start | bytes 2420744 | tf_op jit(solution)/shard_map/while/body/eval_jaxpr/ppermute | solution.py:14
  197.6 1.6 copy-start
  198.1 3.1 copy-start.3
  201.2 39.5 %copy-start.2 = (f32[1024]{0:T(1024)S(1)}, f32[1024]{0:T(1024)}, u32[]{:S(2)}) copy-start(f32[1024]{0:T(1024)} %get-tuple-element.544) | copy-start | bytes 12292 | tf_op jit(solution)/shard_map/while
  216.3 21.2 %collective-permute-start = (f32[1,197,1024]{2,0,1:T(1,128)S(1)}, f32[1,197,1024]{2,0,1:T(1,128)S(1)}, u32[]{:S(2)}, u32[]{:S(2)}) collective-permute-start(f32[1,197,1024]{2,0,1:T(1,128)S(1)} %copy.298), channel_id=1, source_target_pairs={{0,32},{32,64},{64,96},{1,33},{33,65},{65,97},{2,34},{34,66},{66,9... | collective-permute-start | bytes 2420744 | tf_op jit(solution)/shard_map/while/body/eval_jaxpr/ppermute | solution.py:14
  255.3 1.6 copy-start
  255.8 3.1 copy-start.3
  258.9 38.6 %copy-start.2 = (f32[1024]{0:T(1024)S(1)}, f32[1024]{0:T(1024)}, u32[]{:S(2)}) copy-start(f32[1024]{0:T(1024)} %get-tuple-element.544) | copy-start | bytes 12292 | tf_op jit(solution)/shard_map/while
  274.0 20.3 %collective-permute-start = (f32[1,197,1024]{2,0,1:T(1,128)S(1)}, f32[1,197,1024]{2,0,1:T(1,128)S(1)}, u32[]{:S(2)}, u32[]{:S(2)}) collective-permute-start(f32[1,197,1024]{2,0,1:T(1,128)S(1)} %copy.298), channel_id=1, source_target_pairs={{0,32},{32,64},{64,96},{1,33},{33,65},{65,97},{2,34},{34,66},{66,9... | collective-permute-start | bytes 2420744 | tf_op jit(solution)/shard_map/while/body/eval_jaxpr/ppermute | solution.py:14
  312.1 1.6 copy-start
  312.6 3.1 copy-start.3
  315.7 37.7 %copy-start.2 = (f32[1024]{0:T(1024)S(1)}, f32[1024]{0:T(1024)}, u32[]{:S(2)}) copy-start(f32[1024]{0:T(1024)} %get-tuple-element.544) | copy-start | bytes 12292 | tf_op jit(solution)/shard_map/while
  330.8 19.4 %collective-permute-start = (f32[1,197,1024]{2,0,1:T(1,128)S(1)}, f32[1,197,1024]{2,0,1:T(1,128)S(1)}, u32[]{:S(2)}, u32[]{:S(2)}) collective-permute-start(f32[1,197,1024]{2,0,1:T(1,128)S(1)} %copy.298), channel_id=1, source_target_pairs={{0,32},{32,64},{64,96},{1,33},{33,65},{65,97},{2,34},{34,66},{66,9... | collective-permute-start | bytes 2420744 | tf_op jit(solution)/shard_map/while/body/eval_jaxpr/ppermute | solution.py:14
  367.9 1.6 copy-start
  368.4 3.1 copy-start.3
  371.6 36.8 %copy-start.2 = (f32[1024]{0:T(1024)S(1)}, f32[1024]{0:T(1024)}, u32[]{:S(2)}) copy-start(f32[1024]{0:T(1024)} %get-tuple-element.544) | copy-start | bytes 12292 | tf_op jit(solution)/shard_map/while
  386.6 18.5 %collective-permute-start = (f32[1,197,1024]{2,0,1:T(1,128)S(1)}, f32[1,197,1024]{2,0,1:T(1,128)S(1)}, u32[]{:S(2)}, u32[]{:S(2)}) collective-permute-start(f32[1,197,1024]{2,0,1:T(1,128)S(1)} %copy.298), channel_id=1, source_target_pairs={{0,32},{32,64},{64,96},{1,33},{33,65},{65,97},{2,34},{34,66},{66,9... | collective-permute-start | bytes 2420744 | tf_op jit(solution)/shard_map/while/body/eval_jaxpr/ppermute | solution.py:14
  409.9 24.7 %copy-start.13 = (pred[3,3]{0,1:T(4,128)(4,1)S(1)}, pred[3,3]{0,1:T(4,128)(4,1)}, u32[]{:S(2)}) copy-start(pred[3,3]{0,1:T(4,128)(4,1)} %get-tuple-element.379) | copy-start | bytes 31
  410.3 36.9 %copy-start.5 = (pred[3,3]{0,1:T(4,128)(4,1)S(1)}, pred[3,3]{0,1:T(4,128)(4,1)}, u32[]{:S(2)}) copy-start(pred[3,3]{0,1:T(4,128)(4,1)} %get-tuple-element.377) | copy-start | bytes 31
  410.3 37.1 %copy-start.6 = (pred[3,3]{0,1:T(4,128)(4,1)S(1)}, pred[3,3]{0,1:T(4,128)(4,1)}, u32[]{:S(2)}) copy-start(pred[3,3]{0,1:T(4,128)(4,1)} %get-tuple-element.376) | copy-start | bytes 31
  410.3 37.2 %copy-start.7 = (pred[3,3]{0,1:T(4,128)(4,1)S(1)}, pred[3,3]{0,1:T(4,128)(4,1)}, u32[]{:S(2)}) copy-start(pred[3,3]{0,1:T(4,128)(4,1)} %get-tuple-element.375) | copy-start | bytes 31
  410.3 37.4 %copy-start.8 = (pred[3,3]{0,1:T(4,128)(4,1)S(1)}, pred[3,3]{0,1:T(4,128)(4,1)}, u32[]{:S(2)}) copy-start(pred[3,3]{0,1:T(4,128)(4,1)} %get-tuple-element.374) | copy-start | bytes 31
  410.3 37.6 %copy-start.9 = (pred[3,3]{0,1:T(4,128)(4,1)S(1)}, pred[3,3]{0,1:T(4,128)(4,1)}, u32[]{:S(2)}) copy-start(pred[3,3]{0,1:T(4,128)(4,1)} %get-tuple-element.373) | copy-start | bytes 31
  410.3 37.7 %copy-start.10 = (pred[3,3]{0,1:T(4,128)(4,1)S(1)}, pred[3,3]{0,1:T(4,128)(4,1)}, u32[]{:S(2)}) copy-start(pred[3,3]{0,1:T(4,128)(4,1)} %get-tuple-element.372) | copy-start | bytes 31
  410.3 37.9 %copy-start.11 = (pred[3,3]{0,1:T(4,128)(4,1)S(1)}, pred[3,3]{0,1:T(4,128)(4,1)}, u32[]{:S(2)}) copy-start(pred[3,3]{0,1:T(4,128)(4,1)} %get-tuple-element.371) | copy-start | bytes 31
  410.3 38.0 %copy-start.12 = (pred[3,3]{0,1:T(4,128)(4,1)S(1)}, pred[3,3]{0,1:T(4,128)(4,1)}, u32[]{:S(2)}) copy-start(pred[3,3]{0,1:T(4,128)(4,1)} %get-tuple-element.378) | copy-start | bytes 31
  414.1 37.5 %copy-start.1 = (bf16[1024,1024]{1,0:T(8,128)(2,1)S(1)}, bf16[1024,1024]{1,0:T(8,128)(2,1)}, u32[]{:S(2)}) copy-start(bf16[1024,1024]{1,0:T(8,128)(2,1)} %get-tuple-element.554) | copy-start | bytes 6291460
  414.2 20.8 %collective-permute-start.8 = (bf16[3,2048]{1,0:T(4,128)(2,1)S(1)}, bf16[3,2048]{1,0:T(4,128)(2,1)S(1)}, u32[]{:S(2)}, u32[]{:S(2)}) collective-permute-start(bf16[3,2048]{1,0:T(4,128)(2,1)S(1)} %slice.122), channel_id=1, source_target_pairs={{4,0},{5,1},{6,2},{7,3},{8,4},{9,5},{10,6},{11,7},{12,8},{13,9},{1... | collective-permute-start | bytes 36872 | tf_op jit(solution)/shard_map/ppermute | solution.py:14
  418.8 18.1 %collective-permute-start.7 = (bf16[3,2048]{1,0:T(4,128)(2,1)S(1)}, bf16[3,2048]{1,0:T(4,128)(2,1)S(1)}, u32[]{:S(2)}, u32[]{:S(2)}) collective-permute-start(bf16[3,2048]{1,0:T(4,128)(2,1)S(1)} %slice.122), channel_id=1, source_target_pairs={{0,4},{1,5},{2,6},{3,7},{4,8},{5,9},{6,10},{7,11},{8,12},{9,13},{1... | collective-permute-start | bytes 36872 | tf_op jit(solution)/shard_map/ppermute | solution.py:14
  421.7 17.4 %collective-permute-start.6 = (bf16[3,2048]{1,0:T(4,128)(2,1)S(1)}, bf16[3,2048]{1,0:T(4,128)(2,1)S(1)}, u32[]{:S(2)}, u32[]{:S(2)}) collective-permute-start(bf16[3,2048]{1,0:T(4,128)(2,1)S(1)} %slice.122), channel_id=1, source_target_pairs={{3,0},{4,1},{5,2},{6,3},{7,4},{8,5},{9,6},{10,7},{11,8},{12,9},{13... | collective-permute-start | bytes 36872 | tf_op jit(solution)/shard_map/ppermute | solution.py:14
  423.6 17.7 %collective-permute-start.5 = (bf16[3,2048]{1,0:T(4,128)(2,1)S(1)}, bf16[3,2048]{1,0:T(4,128)(2,1)S(1)}, u32[]{:S(2)}, u32[]{:S(2)}) collective-permute-start(bf16[3,2048]{1,0:T(4,128)(2,1)S(1)} %slice.122), channel_id=1, source_target_pairs={{0,3},{1,4},{2,5},{3,6},{4,7},{5,8},{6,9},{7,10},{8,11},{9,12},{10... | collective-permute-start | bytes 36872 | tf_op jit(solution)/shard_map/ppermute | solution.py:14
  427.2 14.0 %collective-permute-start.4 = (bf16[3,2048]{1,0:T(4,128)(2,1)S(1)}, bf16[3,2048]{1,0:T(4,128)(2,1)S(1)}, u32[]{:S(2)}, u32[]{:S(2)}) collective-permute-start(bf16[3,2048]{1,0:T(4,128)(2,1)S(1)} %slice.122), channel_id=1, source_target_pairs={{2,0},{3,1},{4,2},{5,3},{6,4},{7,5},{8,6},{9,7},{10,8},{11,9},{12,... | collective-permute-start | bytes 36872 | tf_op jit(solution)/shard_map/ppermute | solution.py:14
  434.9 7.7 %collective-permute-start.3 = (bf16[3,2048]{1,0:T(4,128)(2,1)S(1)}, bf16[3,2048]{1,0:T(4,128)(2,1)S(1)}, u32[]{:S(2)}, u32[]{:S(2)}) collective-permute-start(bf16[3,2048]{1,0:T(4,128)(2,1)S(1)} %slice.122), channel_id=1, source_target_pairs={{0,2},{1,3},{2,4},{3,5},{4,6},{5,7},{6,8},{7,9},{8,10},{9,11},{10,... | collective-permute-start | bytes 36872 | tf_op jit(solution)/shard_map/ppermute | solution.py:14
  436.9 5.8 %collective-permute-start.2 = (bf16[3,2048]{1,0:T(4,128)(2,1)S(1)}, bf16[3,2048]{1,0:T(4,128)(2,1)S(1)}, u32[]{:S(2)}, u32[]{:S(2)}) collective-permute-start(bf16[3,2048]{1,0:T(4,128)(2,1)S(1)} %slice.122), channel_id=1, source_target_pairs={{1,0},{2,1},{3,2},{4,3},{5,4},{6,5},{7,6},{8,7},{9,8},{10,9},{11,1... | collective-permute-start | bytes 36872 | tf_op jit(solution)/shard_map/ppermute | solution.py:14
  439.1 7.3 %collective-permute-start.1 = (bf16[3,2048]{1,0:T(4,128)(2,1)S(1)}, bf16[3,2048]{1,0:T(4,128)(2,1)S(1)}, u32[]{:S(2)}, u32[]{:S(2)}) collective-permute-start(bf16[3,2048]{1,0:T(4,128)(2,1)S(1)} %slice.122), channel_id=1, source_target_pairs={{0,1},{1,2},{2,3},{3,4},{4,5},{5,6},{6,7},{7,8},{8,9},{9,10},{10,1... | collective-permute-start | bytes 36872 | tf_op jit(solution)/shard_map/ppermute | solution.py:14
  446.8 5.5 %copy-start.4 = (f32[1,1024]{1,0:T(1,128)S(1)}, f32[1,1024]{1,0:T(1,128)}, u32[]{:S(2)}) copy-start(f32[1,1024]{1,0:T(1,128)} %get-tuple-element.582) | copy-start | bytes 12292
Sparse Core Ops, SparseCore 0:
  9.5 61.7 all-gather.4
  73.6 52.9 all-gather.6
where the time goes:
time: 480 us; the launch traced here: 478 us
  waiting for transfers between devices  201 us (42%)
  matrix products  129 us (27%)
  other arithmetic  52.1 us (11%)
  starting transfers between devices  47.8 us (10%)
  local copies, waits for them, and re-layouts  22 us (5%)
  between operations  14.1 us (3%)
  blocking collectives  10.4 us (2%)
    ppermute x13, waiting for transfers between devices, from_behind(): lax.ppermute(value, axis, [(source, source + steps) for source in range(l...  83.6 us
    dot_general x5, matrix products, spatial_layer(): jnp.einsum('gpf,fd->gpd', hidden, reduce_weight, preferred_element_type=j...  71.1 us
    all_gather x1, waiting for transfers between devices, body(): lax.all_gather(expand_weight[0], 'lane', axis=1, tiled=True)  61.2 us
    all_gather x1, waiting for transfers between devices, body(): lax.all_gather(reduce_weight[0], 'lane', axis=0, tiled=True)  55.2 us
    ppermute x13, starting transfers between devices, from_behind(): lax.ppermute(value, axis, [(source, source + steps) for source in range(l...  47.7 us
    dot_general x5, matrix products, spatial_layer(): jnp.einsum('gpd,de->gpe', normed, triple_weight, preferred_element_type=j...  28 us
    reduce_sum x17, other arithmetic, normalize(): spread = jnp.mean(centred * centred, axis=-1, keepdims=True)  18.5 us
    sub x5, other arithmetic, spatial_layer(): weights = jax.nn.softmax(scores, axis=-1).astype(jnp.bfloat16)  13.5 us
  transfers between devices with their start and end apart: 15, of which 9 were waited for; matrix products, arithmetic and copies ran while one was open for 1% of the time, Pallas kernels for 0%

commit v1 on v0

--- a/solution.py
+++ b/solution.py
@@ -165,7 +165,12 @@
     ).astype(jnp.bfloat16)
     temporal = temporal + jnp.dot(hidden, reduce_full, preferred_element_type=jnp.float32)
     columns = temporal.reshape(frame_count, segment_count, model_width // segment_count)
-    shared = lax.all_to_all(columns, "segment", split_axis=1, concat_axis=1, tiled=True)
+    shared = jnp.concatenate(
+        lax.all_to_all(
+            jnp.stack(jnp.split(columns, lax.axis_size("segment"), axis=1)), "segment", 0, 0
+        ),
+        axis=1,
+    )
     return shared[:, segment_count - 1]
 
 

time: 480 us -> 480 us (level)
  no operation moved by 1% of the time
where the time goes in v1:
time: 480 us; the launch traced here: 478 us
  waiting for transfers between devices  201 us (42%)
  matrix products  129 us (27%)
  other arithmetic  52.2 us (11%)
  starting transfers between devices  47.8 us (10%)
  local copies, waits for them, and re-layouts  22.1 us (5%)
  between operations  14.1 us (3%)
  blocking collectives  10.4 us (2%)
    ppermute x13, waiting for transfers between devices, from_behind(): lax.ppermute(value, axis, [(source, source + steps) for source in range(l...  83.6 us
    dot_general x5, matrix products, spatial_layer(): jnp.einsum('gpf,fd->gpd', hidden, reduce_weight, preferred_element_type=j...  71.1 us
    all_gather x1, waiting for transfers between devices, body(): lax.all_gather(expand_weight[0], 'lane', axis=1, tiled=True)  61.2 us
    all_gather x1, waiting for transfers between devices, body(): lax.all_gather(reduce_weight[0], 'lane', axis=0, tiled=True)  55.2 us
    ppermute x13, starting transfers between devices, from_behind(): lax.ppermute(value, axis, [(source, source + steps) for source in range(l...  47.7 us
    dot_general x5, matrix products, spatial_layer(): jnp.einsum('gpd,de->gpe', normed, triple_weight, preferred_element_type=j...  28 us
    reduce_sum x17, other arithmetic, normalize(): spread = jnp.mean(centred * centred, axis=-1, keepdims=True)  18.5 us
    sub x5, other arithmetic, spatial_layer(): weights = jax.nn.softmax(scores, axis=-1).astype(jnp.bfloat16)  13.5 us
  transfers between devices with their start and end apart: 15, of which 9 were waited for; matrix products, arithmetic and copies ran while one was open for 1% of the time, Pallas kernels for 0%

profile of v1, /device:TPU:2, one launch (start us, length us, event | category | flops | bytes accessed | tf_op | source)
XLA Modules:
  0.0 478.4 jit_solution(15995879816722869848)
XLA Ops:
  10.1 61.2 %all-gather.5.cloned.1.call-done = bf16[1,1024,4096]{2,1,0:T(8,128)(2,1)} async-done(((bf16[1,1024,128]{2,1,0:T(8,128)(2,1)}), bf16[1,1024,4096]{2,1,0:T(8,128)(2,1)}) %all-gather.5.cloned.1.call-update) | async-done | bytes 8388624 | tf_op jit(solution)/shard_map/all_gather | solution.py:100
  71.3 55.2 %all-gather.7.cloned.1.call-done = bf16[1,4096,1024]{2,1,0:T(8,128)(2,1)} async-done(((bf16[1,128,1024]{2,1,0:T(8,128)(2,1)}), bf16[1,4096,1024]{2,1,0:T(8,128)(2,1)}) %all-gather.7.cloned.1.call-update) | async-done | bytes 8388624 | tf_op jit(solution)/shard_map/all_gather | solution.py:101
  127.0 283.0 %while.17 = (s32[]{:T(128)}, f32[1,197,1024]{2,0,1:T(1,128)S(1)}, f32[3,1024]{1,0:T(4,128)S(1)}, pred[]{:T(512)}, bf16[3,197,1024]{2,1,0:T(8,128)(2,1)}, /*index...) while((s32[]{:T(128)}, f32[1,197,1024]{2,0,1:T(1,128)S(1)}, ...), condition=%wide.region_10.11_spmd, body=%wide.region_0.10_spmd.sunk | while | flops 5180471808 | bytes 65759924 | solution.py:130
  128.2 1.3 multiply_reduce_fusion.11
  129.5 5.6 %convolution_convert_fusion.3 = bf16[197,3072]{1,0:T(8,128)(2,1)} fusion(bf16[1024,3072]{1,0:T(8,128)(2,1)} %get-tuple-element.543, f32[1024]{0:T(1024)} %bitcast.316, f32[197]{0:T(256)S(1)} %add_rsqrt_fusion.8, f32[197]{0:T(256)S(1)} %broadcast_multiply_fusion.10, f32[1,197,1024]{2,0,1:T(1,128)S(1)} %get-tuple-element.520, ...), kind=kOutput, calls=%fused_computation.2.clone.1 | convolution fusion | flops 1241232384 | bytes 8724524 | tf_op jit(solution)/shard_map/while/body/eval_jaxpr/gpd,de->gpe/dot_general | solution.py:30
  135.1 1.6 copy.350
  137.4 2.7 fusion.341
  141.7 1.7 fusion.343
  143.7 14.2 %fusion.344 = f32[1,197,1024]{2,1,0:T(8,128)S(1)} fusion(f32[1,197,1024]{2,1,0:T(8,128)S(1)} %get-tuple-element.499, bf16[4096,1024]{1,0:T(8,128)(2,1)} %get-tuple-element.547, bf16[1024,4096]{1,0:T(8,128)(2,1)} %get-tuple-element.546, f32[1024]{0:T(1024)S(1)} %bitcast.318, f32[197]{0:T(256)S(1)} %add_rsqrt_fusion.9, ...), kind=kOutput, calls=%fused_computation.61.clone.1 | convolution fusion | flops 3358569472 | bytes 18396712 | tf_op jit(solution)/shard_map/while/body/eval_jaxpr/gpf,fd->gpd/dot_general | solution.py:50
  158.8 3.4 collective-permute-start
  162.2 17.6 %collective-permute-done = f32[1,197,1024]{2,0,1:T(1,128)S(1)} collective-permute-done((f32[1,197,1024]{2,0,1:T(1,128)S(1)}, f32[1,197,1024]{2,0,1:T(1,128)S(1)}, u32[]{:S(2)}, u32[]{:S(2)}) %collective-permute-start) | collective-permute-done | bytes 806944 | tf_op jit(solution)/shard_map/while/body/eval_jaxpr/ppermute | solution.py:14
  180.9 2.1 multiply_reduce_fusion.13
  183.0 1.3 multiply_reduce_fusion.14
  185.7 1.3 multiply_reduce_fusion.11
  187.0 5.6 %convolution_convert_fusion.3 = bf16[197,3072]{1,0:T(8,128)(2,1)} fusion(bf16[1024,3072]{1,0:T(8,128)(2,1)} %get-tuple-element.543, f32[1024]{0:T(1024)} %bitcast.316, f32[197]{0:T(256)S(1)} %add_rsqrt_fusion.8, f32[197]{0:T(256)S(1)} %broadcast_multiply_fusion.10, f32[1,197,1024]{2,0,1:T(1,128)S(1)} %get-tuple-element.520, ...), kind=kOutput, calls=%fused_computation.2.clone.1 | convolution fusion | flops 1241232384 | bytes 8724524 | tf_op jit(solution)/shard_map/while/body/eval_jaxpr/gpd,de->gpe/dot_general | solution.py:30
  192.6 1.6 copy.350
  194.9 2.7 fusion.341
  199.2 1.7 fusion.343
  201.2 14.2 %fusion.344 = f32[1,197,1024]{2,1,0:T(8,128)S(1)} fusion(f32[1,197,1024]{2,1,0:T(8,128)S(1)} %get-tuple-element.499, bf16[4096,1024]{1,0:T(8,128)(2,1)} %get-tuple-element.547, bf16[1024,4096]{1,0:T(8,128)(2,1)} %get-tuple-element.546, f32[1024]{0:T(1024)S(1)} %bitcast.318, f32[197]{0:T(256)S(1)} %add_rsqrt_fusion.9, ...), kind=kOutput, calls=%fused_computation.61.clone.1 | convolution fusion | flops 3358569472 | bytes 18396712 | tf_op jit(solution)/shard_map/while/body/eval_jaxpr/gpf,fd->gpd/dot_general | solution.py:50
  216.3 4.4 collective-permute-start
  220.7 16.8 %collective-permute-done = f32[1,197,1024]{2,0,1:T(1,128)S(1)} collective-permute-done((f32[1,197,1024]{2,0,1:T(1,128)S(1)}, f32[1,197,1024]{2,0,1:T(1,128)S(1)}, u32[]{:S(2)}, u32[]{:S(2)}) %collective-permute-start) | collective-permute-done | bytes 806944 | tf_op jit(solution)/shard_map/while/body/eval_jaxpr/ppermute | solution.py:14
  238.6 2.1 multiply_reduce_fusion.13
  240.8 1.3 multiply_reduce_fusion.14
  243.4 1.3 multiply_reduce_fusion.11
  244.7 5.6 %convolution_convert_fusion.3 = bf16[197,3072]{1,0:T(8,128)(2,1)} fusion(bf16[1024,3072]{1,0:T(8,128)(2,1)} %get-tuple-element.543, f32[1024]{0:T(1024)} %bitcast.316, f32[197]{0:T(256)S(1)} %add_rsqrt_fusion.8, f32[197]{0:T(256)S(1)} %broadcast_multiply_fusion.10, f32[1,197,1024]{2,0,1:T(1,128)S(1)} %get-tuple-element.520, ...), kind=kOutput, calls=%fused_computation.2.clone.1 | convolution fusion | flops 1241232384 | bytes 8724524 | tf_op jit(solution)/shard_map/while/body/eval_jaxpr/gpd,de->gpe/dot_general | solution.py:30
  250.3 1.6 copy.350
  252.6 2.7 fusion.341
  256.9 1.7 fusion.343
  258.9 14.2 %fusion.344 = f32[1,197,1024]{2,1,0:T(8,128)S(1)} fusion(f32[1,197,1024]{2,1,0:T(8,128)S(1)} %get-tuple-element.499, bf16[4096,1024]{1,0:T(8,128)(2,1)} %get-tuple-element.547, bf16[1024,4096]{1,0:T(8,128)(2,1)} %get-tuple-element.546, f32[1024]{0:T(1024)S(1)} %bitcast.318, f32[197]{0:T(256)S(1)} %add_rsqrt_fusion.9, ...), kind=kOutput, calls=%fused_computation.61.clone.1 | convolution fusion | flops 3358569472 | bytes 18396712 | tf_op jit(solution)/shard_map/while/body/eval_jaxpr/gpf,fd->gpd/dot_general | solution.py:50
  274.0 4.4 collective-permute-start
  278.4 15.9 %collective-permute-done = f32[1,197,1024]{2,0,1:T(1,128)S(1)} collective-permute-done((f32[1,197,1024]{2,0,1:T(1,128)S(1)}, f32[1,197,1024]{2,0,1:T(1,128)S(1)}, u32[]{:S(2)}, u32[]{:S(2)}) %collective-permute-start) | collective-permute-done | bytes 806944 | tf_op jit(solution)/shard_map/while/body/eval_jaxpr/ppermute | solution.py:14
  295.4 2.1 multiply_reduce_fusion.13
  297.5 1.3 multiply_reduce_fusion.14
  301.5 5.6 %convolution_convert_fusion.3 = bf16[197,3072]{1,0:T(8,128)(2,1)} fusion(bf16[1024,3072]{1,0:T(8,128)(2,1)} %get-tuple-element.543, f32[1024]{0:T(1024)} %bitcast.316, f32[197]{0:T(256)S(1)} %add_rsqrt_fusion.8, f32[197]{0:T(256)S(1)} %broadcast_multiply_fusion.10, f32[1,197,1024]{2,0,1:T(1,128)S(1)} %get-tuple-element.520, ...), kind=kOutput, calls=%fused_computation.2.clone.1 | convolution fusion | flops 1241232384 | bytes 8724524 | tf_op jit(solution)/shard_map/while/body/eval_jaxpr/gpd,de->gpe/dot_general | solution.py:30
  307.1 1.6 copy.350
  309.4 2.7 fusion.341
  313.7 1.7 fusion.343
  315.7 14.2 %fusion.344 = f32[1,197,1024]{2,1,0:T(8,128)S(1)} fusion(f32[1,197,1024]{2,1,0:T(8,128)S(1)} %get-tuple-element.499, bf16[4096,1024]{1,0:T(8,128)(2,1)} %get-tuple-element.547, bf16[1024,4096]{1,0:T(8,128)(2,1)} %get-tuple-element.546, f32[1024]{0:T(1024)S(1)} %bitcast.318, f32[197]{0:T(256)S(1)} %add_rsqrt_fusion.9, ...), kind=kOutput, calls=%fused_computation.61.clone.1 | convolution fusion | flops 3358569472 | bytes 18396712 | tf_op jit(solution)/shard_map/while/body/eval_jaxpr/gpf,fd->gpd/dot_general | solution.py:50
  330.8 4.4 collective-permute-start
  335.2 14.9 %collective-permute-done = f32[1,197,1024]{2,0,1:T(1,128)S(1)} collective-permute-done((f32[1,197,1024]{2,0,1:T(1,128)S(1)}, f32[1,197,1024]{2,0,1:T(1,128)S(1)}, u32[]{:S(2)}, u32[]{:S(2)}) %collective-permute-start) | collective-permute-done | bytes 806944 | tf_op jit(solution)/shard_map/while/body/eval_jaxpr/ppermute | solution.py:14
  351.3 2.1 multiply_reduce_fusion.13
  353.4 1.3 multiply_reduce_fusion.14
  357.4 5.6 %convolution_convert_fusion.3 = bf16[197,3072]{1,0:T(8,128)(2,1)} fusion(bf16[1024,3072]{1,0:T(8,128)(2,1)} %get-tuple-element.543, f32[1024]{0:T(1024)} %bitcast.316, f32[197]{0:T(256)S(1)} %add_rsqrt_fusion.8, f32[197]{0:T(256)S(1)} %broadcast_multiply_fusion.10, f32[1,197,1024]{2,0,1:T(1,128)S(1)} %get-tuple-element.520, ...), kind=kOutput, calls=%fused_computation.2.clone.1 | convolution fusion | flops 1241232384 | bytes 8724524 | tf_op jit(solution)/shard_map/while/body/eval_jaxpr/gpd,de->gpe/dot_general | solution.py:30
  363.0 1.6 copy.350
  365.2 2.7 fusion.341
  369.5 1.7 fusion.343
  371.6 14.2 %fusion.344 = f32[1,197,1024]{2,1,0:T(8,128)S(1)} fusion(f32[1,197,1024]{2,1,0:T(8,128)S(1)} %get-tuple-element.499, bf16[4096,1024]{1,0:T(8,128)(2,1)} %get-tuple-element.547, bf16[1024,4096]{1,0:T(8,128)(2,1)} %get-tuple-element.546, f32[1024]{0:T(1024)S(1)} %bitcast.318, f32[197]{0:T(256)S(1)} %add_rsqrt_fusion.9, ...), kind=kOutput, calls=%fused_computation.61.clone.1 | convolution fusion | flops 3358569472 | bytes 18396712 | tf_op jit(solution)/shard_map/while/body/eval_jaxpr/gpf,fd->gpd/dot_general | solution.py:50
  386.6 4.4 collective-permute-start
  391.1 14.0 %collective-permute-done = f32[1,197,1024]{2,0,1:T(1,128)S(1)} collective-permute-done((f32[1,197,1024]{2,0,1:T(1,128)S(1)}, f32[1,197,1024]{2,0,1:T(1,128)S(1)}, u32[]{:S(2)}, u32[]{:S(2)}) %collective-permute-start) | collective-permute-done | bytes 806944 | tf_op jit(solution)/shard_map/while/body/eval_jaxpr/ppermute | solution.py:14
  406.2 2.1 multiply_reduce_fusion.13
  408.3 1.3 multiply_reduce_fusion.14
  410.4 3.8 convolution_convert_fusion.1
  414.2 4.6 collective-permute-start.8
  418.8 2.9 collective-permute-start.7
  421.7 1.9 collective-permute-start.6
  423.6 3.6 collective-permute-start.5
  427.2 7.2 %collective-permute-start.4 = (bf16[3,2048]{1,0:T(4,128)(2,1)S(1)}, bf16[3,2048]{1,0:T(4,128)(2,1)S(1)}, u32[]{:S(2)}, u32[]{:S(2)}) collective-permute-start(bf16[3,2048]{1,0:T(4,128)(2,1)S(1)} %slice.122), channel_id=1, source_target_pairs={{2,0},{3,1},{4,2},{5,3},{6,4},{7,5},{8,6},{9,7},{10,8},{11,9},{12,... | collective-permute-start | bytes 36872 | tf_op jit(solution)/shard_map/ppermute | solution.py:14
  434.9 1.9 collective-permute-start.3
  436.9 2.2 collective-permute-start.2
  439.1 2.2 collective-permute-start.1
  441.3 1.3 collective-permute-done.3
  443.3 3.1 collective-permute-done.1
  452.4 8.1 %convolution_add_fusion = f32[3,1024]{1,0:T(4,128)S(1)} fusion(f32[3,1024]{1,0:T(4,128)S(1)} %get-tuple-element.403, f32[1024]{0:T(1024)S(1)} %bitcast.319, f32[3]{0:T(128)S(1)} %add_rsqrt_fusion.3, f32[3]{0:T(128)S(1)} %broadcast_multiply_fusion.4, bf16[1,4096,1024]{2,1,0:T(8,128)(2,1)} %bitcast.310, bf16[1,1024,4096]{2,1,0:T(8,128)(2,1)} %bitcast.308), kind=kOutput, calls=%fused_computation.161 | convolution fusion | flops 51145728 | bytes 16805912 | tf_op jit(solution)/shard_map/dot_general | solution.py:166
  460.5 10.4 %all_to_all.5 = f32[4,3,1,256]{3,2,1,0:T(1,128)S(1)} all-to-all(f32[4,3,1,256]{3,2,1,0:T(1,128)S(1)} %pad_maximum_fusion), channel_id=1, replica_groups=mesh['segment'=4,'lane'=32] {'segment'}, dimensions={0} | all-to-all | bytes 24576 | tf_op jit(solution)/shard_map/all_to_all | solution.py:169
  (231 shorter events, 42.9 us)
Async XLA Ops:
  6.5 64.8 %all-gather.5.cloned.1.call-start = ((), (), s32[]{:S(2)}) async-start(), calls=%async_computation.1 | async-start | bytes 8650752 | tf_op jit(solution)/shard_map/all_gather | solution.py:100
  7.3 119.3 %all-gather.7.cloned.1.call-start = ((), (), s32[]{:S(2)}) async-start(), calls=%async_computation.2 | async-start | bytes 8650752 | tf_op jit(solution)/shard_map/all_gather | solution.py:101
  140.1 1.6 copy-start
  140.6 3.1 copy-start.3
  143.7 39.3 %copy-start.2 = (f32[1024]{0:T(1024)S(1)}, f32[1024]{0:T(1024)}, u32[]{:S(2)}) copy-start(f32[1024]{0:T(1024)} %get-tuple-element.548) | copy-start | bytes 12292 | tf_op jit(solution)/shard_map/while
  158.8 21.1 %collective-permute-start = (f32[1,197,1024]{2,0,1:T(1,128)S(1)}, f32[1,197,1024]{2,0,1:T(1,128)S(1)}, u32[]{:S(2)}, u32[]{:S(2)}) collective-permute-start(f32[1,197,1024]{2,0,1:T(1,128)S(1)} %copy.351), channel_id=1, source_target_pairs={{0,32},{32,64},{64,96},{1,33},{33,65},{65,97},{2,34},{34,66},{66,9... | collective-permute-start | bytes 2420744 | tf_op jit(solution)/shard_map/while/body/eval_jaxpr/ppermute | solution.py:14
  197.6 1.6 copy-start
  198.1 3.1 copy-start.3
  201.2 39.5 %copy-start.2 = (f32[1024]{0:T(1024)S(1)}, f32[1024]{0:T(1024)}, u32[]{:S(2)}) copy-start(f32[1024]{0:T(1024)} %get-tuple-element.548) | copy-start | bytes 12292 | tf_op jit(solution)/shard_map/while
  216.3 21.2 %collective-permute-start = (f32[1,197,1024]{2,0,1:T(1,128)S(1)}, f32[1,197,1024]{2,0,1:T(1,128)S(1)}, u32[]{:S(2)}, u32[]{:S(2)}) collective-permute-start(f32[1,197,1024]{2,0,1:T(1,128)S(1)} %copy.351), channel_id=1, source_target_pairs={{0,32},{32,64},{64,96},{1,33},{33,65},{65,97},{2,34},{34,66},{66,9... | collective-permute-start | bytes 2420744 | tf_op jit(solution)/shard_map/while/body/eval_jaxpr/ppermute | solution.py:14
  255.3 1.6 copy-start
  255.8 3.1 copy-start.3
  258.9 38.6 %copy-start.2 = (f32[1024]{0:T(1024)S(1)}, f32[1024]{0:T(1024)}, u32[]{:S(2)}) copy-start(f32[1024]{0:T(1024)} %get-tuple-element.548) | copy-start | bytes 12292 | tf_op jit(solution)/shard_map/while
  274.0 20.3 %collective-permute-start = (f32[1,197,1024]{2,0,1:T(1,128)S(1)}, f32[1,197,1024]{2,0,1:T(1,128)S(1)}, u32[]{:S(2)}, u32[]{:S(2)}) collective-permute-start(f32[1,197,1024]{2,0,1:T(1,128)S(1)} %copy.351), channel_id=1, source_target_pairs={{0,32},{32,64},{64,96},{1,33},{33,65},{65,97},{2,34},{34,66},{66,9... | collective-permute-start | bytes 2420744 | tf_op jit(solution)/shard_map/while/body/eval_jaxpr/ppermute | solution.py:14
  312.1 1.6 copy-start
  312.6 3.1 copy-start.3
  315.7 37.7 %copy-start.2 = (f32[1024]{0:T(1024)S(1)}, f32[1024]{0:T(1024)}, u32[]{:S(2)}) copy-start(f32[1024]{0:T(1024)} %get-tuple-element.548) | copy-start | bytes 12292 | tf_op jit(solution)/shard_map/while
  330.8 19.4 %collective-permute-start = (f32[1,197,1024]{2,0,1:T(1,128)S(1)}, f32[1,197,1024]{2,0,1:T(1,128)S(1)}, u32[]{:S(2)}, u32[]{:S(2)}) collective-permute-start(f32[1,197,1024]{2,0,1:T(1,128)S(1)} %copy.351), channel_id=1, source_target_pairs={{0,32},{32,64},{64,96},{1,33},{33,65},{65,97},{2,34},{34,66},{66,9... | collective-permute-start | bytes 2420744 | tf_op jit(solution)/shard_map/while/body/eval_jaxpr/ppermute | solution.py:14
  367.9 1.6 copy-start
  368.4 3.1 copy-start.3
  371.6 36.8 %copy-start.2 = (f32[1024]{0:T(1024)S(1)}, f32[1024]{0:T(1024)}, u32[]{:S(2)}) copy-start(f32[1024]{0:T(1024)} %get-tuple-element.548) | copy-start | bytes 12292 | tf_op jit(solution)/shard_map/while
  386.6 18.5 %collective-permute-start = (f32[1,197,1024]{2,0,1:T(1,128)S(1)}, f32[1,197,1024]{2,0,1:T(1,128)S(1)}, u32[]{:S(2)}, u32[]{:S(2)}) collective-permute-start(f32[1,197,1024]{2,0,1:T(1,128)S(1)} %copy.351), channel_id=1, source_target_pairs={{0,32},{32,64},{64,96},{1,33},{33,65},{65,97},{2,34},{34,66},{66,9... | collective-permute-start | bytes 2420744 | tf_op jit(solution)/shard_map/while/body/eval_jaxpr/ppermute | solution.py:14
  409.9 24.7 %copy-start.13 = (pred[3,3]{0,1:T(4,128)(4,1)S(1)}, pred[3,3]{0,1:T(4,128)(4,1)}, u32[]{:S(2)}) copy-start(pred[3,3]{0,1:T(4,128)(4,1)} %get-tuple-element.383) | copy-start | bytes 31
  410.3 36.9 %copy-start.5 = (pred[3,3]{0,1:T(4,128)(4,1)S(1)}, pred[3,3]{0,1:T(4,128)(4,1)}, u32[]{:S(2)}) copy-start(pred[3,3]{0,1:T(4,128)(4,1)} %get-tuple-element.381) | copy-start | bytes 31
  410.3 37.1 %copy-start.6 = (pred[3,3]{0,1:T(4,128)(4,1)S(1)}, pred[3,3]{0,1:T(4,128)(4,1)}, u32[]{:S(2)}) copy-start(pred[3,3]{0,1:T(4,128)(4,1)} %get-tuple-element.380) | copy-start | bytes 31
  410.3 37.2 %copy-start.7 = (pred[3,3]{0,1:T(4,128)(4,1)S(1)}, pred[3,3]{0,1:T(4,128)(4,1)}, u32[]{:S(2)}) copy-start(pred[3,3]{0,1:T(4,128)(4,1)} %get-tuple-element.379) | copy-start | bytes 31
  410.3 37.4 %copy-start.8 = (pred[3,3]{0,1:T(4,128)(4,1)S(1)}, pred[3,3]{0,1:T(4,128)(4,1)}, u32[]{:S(2)}) copy-start(pred[3,3]{0,1:T(4,128)(4,1)} %get-tuple-element.378) | copy-start | bytes 31
  410.3 37.6 %copy-start.9 = (pred[3,3]{0,1:T(4,128)(4,1)S(1)}, pred[3,3]{0,1:T(4,128)(4,1)}, u32[]{:S(2)}) copy-start(pred[3,3]{0,1:T(4,128)(4,1)} %get-tuple-element.377) | copy-start | bytes 31
  410.3 37.7 %copy-start.10 = (pred[3,3]{0,1:T(4,128)(4,1)S(1)}, pred[3,3]{0,1:T(4,128)(4,1)}, u32[]{:S(2)}) copy-start(pred[3,3]{0,1:T(4,128)(4,1)} %get-tuple-element.376) | copy-start | bytes 31
  410.3 37.9 %copy-start.11 = (pred[3,3]{0,1:T(4,128)(4,1)S(1)}, pred[3,3]{0,1:T(4,128)(4,1)}, u32[]{:S(2)}) copy-start(pred[3,3]{0,1:T(4,128)(4,1)} %get-tuple-element.375) | copy-start | bytes 31
  410.3 38.0 %copy-start.12 = (pred[3,3]{0,1:T(4,128)(4,1)S(1)}, pred[3,3]{0,1:T(4,128)(4,1)}, u32[]{:S(2)}) copy-start(pred[3,3]{0,1:T(4,128)(4,1)} %get-tuple-element.382) | copy-start | bytes 31
  414.1 37.5 %copy-start.1 = (bf16[1024,1024]{1,0:T(8,128)(2,1)S(1)}, bf16[1024,1024]{1,0:T(8,128)(2,1)}, u32[]{:S(2)}) copy-start(bf16[1024,1024]{1,0:T(8,128)(2,1)} %get-tuple-element.558) | copy-start | bytes 6291460
  414.2 20.8 %collective-permute-start.8 = (bf16[3,2048]{1,0:T(4,128)(2,1)S(1)}, bf16[3,2048]{1,0:T(4,128)(2,1)S(1)}, u32[]{:S(2)}, u32[]{:S(2)}) collective-permute-start(bf16[3,2048]{1,0:T(4,128)(2,1)S(1)} %slice.122), channel_id=1, source_target_pairs={{4,0},{5,1},{6,2},{7,3},{8,4},{9,5},{10,6},{11,7},{12,8},{13,9},{1... | collective-permute-start | bytes 36872 | tf_op jit(solution)/shard_map/ppermute | solution.py:14
  418.8 18.1 %collective-permute-start.7 = (bf16[3,2048]{1,0:T(4,128)(2,1)S(1)}, bf16[3,2048]{1,0:T(4,128)(2,1)S(1)}, u32[]{:S(2)}, u32[]{:S(2)}) collective-permute-start(bf16[3,2048]{1,0:T(4,128)(2,1)S(1)} %slice.122), channel_id=1, source_target_pairs={{0,4},{1,5},{2,6},{3,7},{4,8},{5,9},{6,10},{7,11},{8,12},{9,13},{1... | collective-permute-start | bytes 36872 | tf_op jit(solution)/shard_map/ppermute | solution.py:14
  421.7 17.4 %collective-permute-start.6 = (bf16[3,2048]{1,0:T(4,128)(2,1)S(1)}, bf16[3,2048]{1,0:T(4,128)(2,1)S(1)}, u32[]{:S(2)}, u32[]{:S(2)}) collective-permute-start(bf16[3,2048]{1,0:T(4,128)(2,1)S(1)} %slice.122), channel_id=1, source_target_pairs={{3,0},{4,1},{5,2},{6,3},{7,4},{8,5},{9,6},{10,7},{11,8},{12,9},{13... | collective-permute-start | bytes 36872 | tf_op jit(solution)/shard_map/ppermute | solution.py:14
  423.6 17.7 %collective-permute-start.5 = (bf16[3,2048]{1,0:T(4,128)(2,1)S(1)}, bf16[3,2048]{1,0:T(4,128)(2,1)S(1)}, u32[]{:S(2)}, u32[]{:S(2)}) collective-permute-start(bf16[3,2048]{1,0:T(4,128)(2,1)S(1)} %slice.122), channel_id=1, source_target_pairs={{0,3},{1,4},{2,5},{3,6},{4,7},{5,8},{6,9},{7,10},{8,11},{9,12},{10... | collective-permute-start | bytes 36872 | tf_op jit(solution)/shard_map/ppermute | solution.py:14
  427.2 14.0 %collective-permute-start.4 = (bf16[3,2048]{1,0:T(4,128)(2,1)S(1)}, bf16[3,2048]{1,0:T(4,128)(2,1)S(1)}, u32[]{:S(2)}, u32[]{:S(2)}) collective-permute-start(bf16[3,2048]{1,0:T(4,128)(2,1)S(1)} %slice.122), channel_id=1, source_target_pairs={{2,0},{3,1},{4,2},{5,3},{6,4},{7,5},{8,6},{9,7},{10,8},{11,9},{12,... | collective-permute-start | bytes 36872 | tf_op jit(solution)/shard_map/ppermute | solution.py:14
  434.9 7.7 %collective-permute-start.3 = (bf16[3,2048]{1,0:T(4,128)(2,1)S(1)}, bf16[3,2048]{1,0:T(4,128)(2,1)S(1)}, u32[]{:S(2)}, u32[]{:S(2)}) collective-permute-start(bf16[3,2048]{1,0:T(4,128)(2,1)S(1)} %slice.122), channel_id=1, source_target_pairs={{0,2},{1,3},{2,4},{3,5},{4,6},{5,7},{6,8},{7,9},{8,10},{9,11},{10,... | collective-permute-start | bytes 36872 | tf_op jit(solution)/shard_map/ppermute | solution.py:14
  436.9 5.8 %collective-permute-start.2 = (bf16[3,2048]{1,0:T(4,128)(2,1)S(1)}, bf16[3,2048]{1,0:T(4,128)(2,1)S(1)}, u32[]{:S(2)}, u32[]{:S(2)}) collective-permute-start(bf16[3,2048]{1,0:T(4,128)(2,1)S(1)} %slice.122), channel_id=1, source_target_pairs={{1,0},{2,1},{3,2},{4,3},{5,4},{6,5},{7,6},{8,7},{9,8},{10,9},{11,1... | collective-permute-start | bytes 36872 | tf_op jit(solution)/shard_map/ppermute | solution.py:14
  439.1 7.3 %collective-permute-start.1 = (bf16[3,2048]{1,0:T(4,128)(2,1)S(1)}, bf16[3,2048]{1,0:T(4,128)(2,1)S(1)}, u32[]{:S(2)}, u32[]{:S(2)}) collective-permute-start(bf16[3,2048]{1,0:T(4,128)(2,1)S(1)} %slice.122), channel_id=1, source_target_pairs={{0,1},{1,2},{2,3},{3,4},{4,5},{5,6},{6,7},{7,8},{8,9},{9,10},{10,1... | collective-permute-start | bytes 36872 | tf_op jit(solution)/shard_map/ppermute | solution.py:14
  446.8 5.5 %copy-start.4 = (f32[1,1024]{1,0:T(1,128)S(1)}, f32[1,1024]{1,0:T(1,128)}, u32[]{:S(2)}) copy-start(f32[1,1024]{1,0:T(1,128)} %get-tuple-element.586) | copy-start | bytes 12292
Sparse Core Ops, SparseCore 0:
  9.5 61.7 all-gather.4
  73.6 52.9 all-gather.6
